TPU v7x, 32 devices: a whole 2x2x4 slice. The times are simulated.
32 devices in a mesh: grp: 2 (over x), chan: 16 (over z, y, core).
Axes of the slice: x: 2, y: 2, z: 4, core: 2. Of those that a mesh axis runs over, the one named last changes fastest.
Arguments:
- traces: bfloat16 [32, 16, 256, 512], P(('grp', 'chan')), parts along dimension 0, may hold values from -6 to 6
- mask: int32 [32, 16], P('grp'), parts along dimension 0, may hold values 0 or 1
- counts: int32 [32], P('grp'), parts along dimension 0, may hold values from 0 to 5, as said below
Outputs:
- forward: float32 [32, 5, 128, 512], P(('grp', 'chan')), parts along dimension 0
- backward: float32 [32, 5, 128, 512], P(('grp', 'chan')), parts along dimension 0
There are 2 independent parts, one for each index of `grp`. A program takes and returns all parts, laid end to end along the dimension named above; each array names one. Nothing has to cross between parts.
Inputs may be any that keep to these rules, and one draw needn't show every extreme that they name: counts[b] <= min(5, 15 - b); block 0 always has 5 partners.
All inputs are finite; a program needn't handle non-finite values.
Results may differ from a plain program's by a relative error of at most 0.0063.
Values may be sent and summed in bfloat16 or wider, within the bound.
A program may use at most 128 MiB of HBM per device.

v0:
```python
import math

import jax
import jax.numpy as jnp
from jax import lax
from jax.sharding import PartitionSpec as P

MAXP = 5


def from_behind(shard, axis, by):
    peers = lax.axis_size(axis)
    pairs = [(i, i + by) for i in range(peers) if 0 <= i + by < peers]
    return lax.ppermute(shard, axis, pairs)


def lag_table(lags, bins):
    times = jnp.arange(lags, dtype=jnp.int32)[:, None]
    freqs = jnp.arange(1, bins + 1, dtype=jnp.int32)[None, :]
    phase = (times * freqs % lags).astype(jnp.float32) * (2.0 * math.pi / lags)
    return jnp.concatenate([jnp.cos(phase), -jnp.sin(phase)], axis=1).astype(jnp.bfloat16)


def whiten(record, table):
    bins = table.shape[1] // 2
    raw = jnp.einsum("tk,wtc->wkc", table, record, preferred_element_type=jnp.float32)
    power = jnp.sum(raw * raw, axis=1) / bins
    return (raw / jnp.sqrt(power + 1e-06)[:, None, :]).astype(jnp.bfloat16)


def stack_pair(first, second, weight):
    half = first.shape[1] // 2
    wlen = first.shape[0]
    first_re = first[:, :half].astype(jnp.float32)
    first_im = first[:, half:].astype(jnp.float32)
    second_re = second[:, :half].astype(jnp.float32)
    second_im = second[:, half:].astype(jnp.float32)
    scaled = weight[:, None, None]
    real_part = jnp.sum(scaled * (first_re * second_re + first_im * second_im), axis=0)
    imag_part = jnp.sum(scaled * (first_im * second_re - first_re * second_im), axis=0)
    return (jnp.concatenate([real_part, imag_part], axis=0) / math.sqrt(wlen)).astype(jnp.bfloat16)


def pair_lags(first, second, weight, table, bins):
    stacked = stack_pair(first, second, weight)
    return jnp.dot(table, stacked, preferred_element_type=jnp.float32) / math.sqrt(bins)


def pick_row(values, index):
    return lax.dynamic_index_in_dim(values, index, 0, keepdims=False)


def local(traces, mask, counts):
    myself = lax.axis_index("chan")
    blocks = mask.shape[0]
    record = traces[0]
    lags = record.shape[1]
    width = record.shape[2]
    bins = lags // 2
    table = lag_table(lags, bins)
    white = whiten(record, table)
    valid = mask.astype(jnp.float32)
    own_valid = pick_row(valid, myself)
    own_count = pick_row(counts, myself)
    zero_lags = jnp.zeros((lags, width), jnp.float32)
    forward_list = []
    backward_list = []
    for step in range(1, MAXP + 1):
        partner = from_behind(white, "chan", -step)
        other = jnp.minimum(myself + step, blocks - 1)
        weight = own_valid * pick_row(valid, other)
        corr = lax.cond(
            own_count >= step,
            lambda: pair_lags(white, partner, weight, table, bins),
            lambda: zero_lags,
        )
        forward_list.append(corr[:bins])
        returned = from_behind(corr[bins:][::-1], "chan", step)
        backward_list.append(returned)
    forward = jnp.stack(forward_list)[None]
    backward = jnp.stack(backward_list)[None]
    return (forward, backward)


def solution(mesh):
    return jax.shard_map(
        local,
        mesh=mesh,
        in_specs=(P(("grp", "chan"), None, None, None), P("grp", None), P("grp")),
        out_specs=(P(("grp", "chan"), None, None, None), P(("grp", "chan"), None, None, None)),
        check_vma=False,
    )
```

profile of v0, /device:TPU:5, one launch (start us, length us, event | category | flops | bytes accessed | tf_op | source)
XLA Modules:
  0.0 475.2 jit_solution(1164922830686994316)
XLA Ops:
  1.3 3.5 multiply_reduce_fusion
  4.8 3.3 fusion.62
  8.0 1.9 collective-permute-start.1
  10.0 2.6 collective-permute-start
  12.6 1.9 collective-permute-start.2
  14.5 1.3 collective-permute-start.3
  15.8 1.3 collective-permute-start.4
  21.0 81.6 %collective-permute-done.1 = bf16[16,256,512]{2,1,0:T(8,128)(2,1)} collective-permute-done((bf16[16,256,512]{2,1,0:T(8,128)(2,1)}, bf16[16,256,512]{2,1,0:T(8,128)(2,1)}, u32[]{:S(2)}, u32[]{:S(2)}) %collective-permute-start.1) | collective-permute-done | bytes 4194336 | tf_op jit(solution)/shard_map/ppermute | solution.py:14
  103.0 7.0 %collective-permute-start.6 = (f32[128,512]{1,0:T(8,128)S(1)}, f32[128,512]{1,0:T(8,128)S(1)}, u32[]{:S(2)}, u32[]{:S(2)}) collective-permute-start(f32[128,512]{1,0:T(8,128)S(1)} %rev.16), channel_id=1, source_target_pairs={{0,2},{1,3},{2,4},{3,5},{4,6},{5,7},{6,8},{7,9},{8,10},{9,11},{10,... | collective-permute-start | bytes 786440 | tf_op jit(solution)/shard_map/ppermute | solution.py:14
  109.9 84.6 %collective-permute-done = bf16[16,256,512]{2,1,0:T(8,128)(2,1)} collective-permute-done((bf16[16,256,512]{2,1,0:T(8,128)(2,1)}, bf16[16,256,512]{2,1,0:T(8,128)(2,1)}, u32[]{:S(2)}, u32[]{:S(2)}) %collective-permute-start) | collective-permute-done | bytes 4194336 | tf_op jit(solution)/shard_map/ppermute | solution.py:14
  194.5 4.7 conditional.5
  194.5 4.5 fusion.2
  199.6 1.9 collective-permute-start.5
  201.9 11.4 %collective-permute-start.7 = (f32[128,512]{1,0:T(8,128)S(1)}, f32[128,512]{1,0:T(8,128)}, u32[]{:S(2)}, u32[]{:S(2)}) collective-permute-start(f32[128,512]{1,0:T(8,128)S(1)} %rev.17), channel_id=1, source_target_pairs={{0,3},{1,4},{2,5},{3,6},{4,7},{5,8},{6,9},{7,10},{8,11},{9,12},{10... | collective-permute-start | bytes 786440 | tf_op jit(solution)/shard_map/ppermute | solution.py:14
  213.6 1.3 rev.18
  214.9 5.8 %collective-permute-start.8 = (f32[128,512]{1,0:T(8,128)}, f32[128,512]{1,0:T(8,128)}, u32[]{:S(2)}, u32[]{:S(2)}) collective-permute-start(f32[128,512]{1,0:T(8,128)} %rev.18), channel_id=1, source_target_pairs={{0,4},{1,5},{2,6},{3,7},{4,8},{5,9},{6,10},{7,11},{8,12},{9,13},{1... | collective-permute-start | bytes 786440 | tf_op jit(solution)/shard_map/ppermute | solution.py:14
  220.7 243.4 %collective-permute-done.4 = bf16[16,256,512]{2,1,0:T(8,128)(2,1)} collective-permute-done((bf16[16,256,512]{2,1,0:T(8,128)(2,1)}, bf16[16,256,512]{2,1,0:T(8,128)(2,1)}, u32[]{:S(2)}, u32[]{:S(2)}) %collective-permute-start.4) | collective-permute-done | bytes 4194336 | tf_op jit(solution)/shard_map/ppermute | solution.py:14
  464.4 2.5 collective-permute-start.9
  468.1 0.7 bitcast_dynamic-update-slice_fusion.8
  470.4 0.7 bitcast_dynamic-update-slice_fusion.5
  471.2 1.0 bitcast_dynamic-update-slice_fusion.2
  472.2 1.0 bitcast_dynamic-update-slice_fusion.1
  473.2 1.0 bitcast_dynamic-update-slice_fusion
  474.2 1.0 copy-done
  (53 shorter events, 6.1 us)
Async XLA Ops:
  4.7 12.3 %copy-start.1 = (s32[16,16]{1,0:T(8,128)S(1)}, s32[16,16]{1,0:T(8,128)}, u32[]{:S(2)}) copy-start(s32[16,16]{1,0:T(8,128)} %param.14) | copy-start | bytes 3076
  4.8 12.4 %copy-start.2 = (s32[16]{0:T(128)S(1)}, s32[16]{0:T(128)}, u32[]{:S(2)}) copy-start(s32[16]{0:T(128)} %param.15) | copy-start | bytes 196
  8.0 94.5 %collective-permute-start.1 = (bf16[16,256,512]{2,1,0:T(8,128)(2,1)}, bf16[16,256,512]{2,1,0:T(8,128)(2,1)}, u32[]{:S(2)}, u32[]{:S(2)}) collective-permute-start(bf16[16,256,512]{2,1,0:T(8,128)(2,1)} %fusion.62), channel_id=1, source_target_pairs={{2,0},{3,1},{4,2},{5,3},{6,4},{7,5},{8,6},{9,7},{10,8},{11,9},{12,... | collective-permute-start | bytes 12582920 | tf_op jit(solution)/shard_map/ppermute | solution.py:14
  10.0 184.6 %collective-permute-start = (bf16[16,256,512]{2,1,0:T(8,128)(2,1)}, bf16[16,256,512]{2,1,0:T(8,128)(2,1)}, u32[]{:S(2)}, u32[]{:S(2)}) collective-permute-start(bf16[16,256,512]{2,1,0:T(8,128)(2,1)} %fusion.62), channel_id=1, source_target_pairs={{1,0},{2,1},{3,2},{4,3},{5,4},{6,5},{7,6},{8,7},{9,8},{10,9},{11,1... | collective-permute-start | bytes 12582920 | tf_op jit(solution)/shard_map/ppermute | solution.py:14
  12.6 189.0 %collective-permute-start.2 = (bf16[16,256,512]{2,1,0:T(8,128)(2,1)}, bf16[16,256,512]{2,1,0:T(8,128)(2,1)}, u32[]{:S(2)}, u32[]{:S(2)}) collective-permute-start(bf16[16,256,512]{2,1,0:T(8,128)(2,1)} %fusion.62), channel_id=1, source_target_pairs={{3,0},{4,1},{5,2},{6,3},{7,4},{8,5},{9,6},{10,7},{11,8},{12,9},{13... | collective-permute-start | bytes 12582920 | tf_op jit(solution)/shard_map/ppermute | solution.py:14
  14.5 198.8 %collective-permute-start.3 = (bf16[16,256,512]{2,1,0:T(8,128)(2,1)}, bf16[16,256,512]{2,1,0:T(8,128)(2,1)}, u32[]{:S(2)}, u32[]{:S(2)}) collective-permute-start(bf16[16,256,512]{2,1,0:T(8,128)(2,1)} %fusion.62), channel_id=1, source_target_pairs={{4,0},{5,1},{6,2},{7,3},{8,4},{9,5},{10,6},{11,7},{12,8},{13,9},{1... | collective-permute-start | bytes 12582920 | tf_op jit(solution)/shard_map/ppermute | solution.py:14
  15.8 448.2 %collective-permute-start.4 = (bf16[16,256,512]{2,1,0:T(8,128)(2,1)}, bf16[16,256,512]{2,1,0:T(8,128)(2,1)}, u32[]{:S(2)}, u32[]{:S(2)}) collective-permute-start(bf16[16,256,512]{2,1,0:T(8,128)(2,1)} %fusion.62), channel_id=1, source_target_pairs={{5,0},{6,1},{7,2},{8,3},{9,4},{10,5},{11,6},{12,7},{13,8},{14,9},{... | collective-permute-start | bytes 12582920 | tf_op jit(solution)/shard_map/ppermute | solution.py:14
  103.0 368.2 %collective-permute-start.6 = (f32[128,512]{1,0:T(8,128)S(1)}, f32[128,512]{1,0:T(8,128)S(1)}, u32[]{:S(2)}, u32[]{:S(2)}) collective-permute-start(f32[128,512]{1,0:T(8,128)S(1)} %rev.16), channel_id=1, source_target_pairs={{0,2},{1,3},{2,4},{3,5},{4,6},{5,7},{6,8},{7,9},{8,10},{9,11},{10,... | collective-permute-start | bytes 786440 | tf_op jit(solution)/shard_map/ppermute | solution.py:14
  199.6 271.6 %collective-permute-start.5 = (f32[128,512]{1,0:T(8,128)S(1)}, f32[128,512]{1,0:T(8,128)S(1)}, u32[]{:S(2)}, u32[]{:S(2)}) collective-permute-start(f32[128,512]{1,0:T(8,128)S(1)} %rev.15), channel_id=1, source_target_pairs={{0,1},{1,2},{2,3},{3,4},{4,5},{5,6},{6,7},{7,8},{8,9},{9,10},{10,1... | collective-permute-start | bytes 786440 | tf_op jit(solution)/shard_map/ppermute | solution.py:14
  201.9 269.3 %collective-permute-start.7 = (f32[128,512]{1,0:T(8,128)S(1)}, f32[128,512]{1,0:T(8,128)}, u32[]{:S(2)}, u32[]{:S(2)}) collective-permute-start(f32[128,512]{1,0:T(8,128)S(1)} %rev.17), channel_id=1, source_target_pairs={{0,3},{1,4},{2,5},{3,6},{4,7},{5,8},{6,9},{7,10},{8,11},{9,12},{10... | collective-permute-start | bytes 786440 | tf_op jit(solution)/shard_map/ppermute | solution.py:14
  214.9 257.3 %collective-permute-start.8 = (f32[128,512]{1,0:T(8,128)}, f32[128,512]{1,0:T(8,128)}, u32[]{:S(2)}, u32[]{:S(2)}) collective-permute-start(f32[128,512]{1,0:T(8,128)} %rev.18), channel_id=1, source_target_pairs={{0,4},{1,5},{2,6},{3,7},{4,8},{5,9},{6,10},{7,11},{8,12},{9,13},{1... | collective-permute-start | bytes 786440 | tf_op jit(solution)/shard_map/ppermute | solution.py:14
  464.4 8.8 %collective-permute-start.9 = (f32[128,512]{1,0:T(8,128)S(1)}, f32[128,512]{1,0:T(8,128)}, u32[]{:S(2)}, u32[]{:S(2)}) collective-permute-start(f32[128,512]{1,0:T(8,128)S(1)} %rev.19), channel_id=1, source_target_pairs={{0,5},{1,6},{2,7},{3,8},{4,9},{5,10},{6,11},{7,12},{8,13},{9,14},{... | collective-permute-start | bytes 786440 | tf_op jit(solution)/shard_map/ppermute | solution.py:14
  474.2 1.1 copy-start
where the time goes:
time: 476 us; the launch traced here: 475 us
  waiting for transfers between devices  410 us (86%)
  starting transfers between devices  37.5 us (8%)
  local copies, waits for them, and re-layouts  11.7 us (2%)
  other arithmetic  8.38 us (2%)
    ppermute x10, waiting for transfers between devices, from_behind(): return lax.ppermute(shard, axis, pairs)  410 us
    ppermute x10, starting transfers between devices, from_behind(): return lax.ppermute(shard, axis, pairs)  37.5 us
  transfers between devices with their start and end apart: 10, of which 3 were waited for; matrix products, arithmetic and copies ran while one was open for 3% of the time, Pallas kernels for 0%

commit v1 on v0

v1 whole, which is shorter than its diff:
```python
import functools
import math

import numpy as np

import jax
import jax.numpy as jnp
from jax import lax
from jax.experimental import pallas as pl
from jax.experimental.pallas import tpu as pltpu
from jax.sharding import PartitionSpec as P

MAXP = 5
TEAM = 4
LANES = 128
GROUPS = 4
SLOTS = 9
TILE = 32

OWN_PAIRS = [(2, 3, 3), (3, 4, 2), (4, 5, 1)]
A_PAIRS = [(0, 2, 4), (1, 2, 4)]
B_PAIRS = [(2, 6, 2), (3, 6, 3)]
AB_PAIRS = [(1, 6, 1)]
FIRST = {}
for _runs in (OWN_PAIRS, A_PAIRS, B_PAIRS, AB_PAIRS):
    for _run in _runs:
        FIRST[_run] = sum(r[2] for r in FIRST)
PAIRS = sum(r[2] for r in FIRST)


def lag_table(lags, bins):
    times = np.arange(lags, dtype=np.int32)[:, None]
    freqs = np.arange(1, bins + 1, dtype=np.int32)[None, :]
    phase = (times * freqs % lags).astype(np.float32) * np.float32(2.0 * math.pi / lags)
    return np.concatenate([np.cos(phase), -np.sin(phase)], axis=1)


def kernel(axis, n, traces, mask, counts, table_t, table_lag, fwd_out, bwd_out,
           record, white, acc, res, back,
           t_send, t_recv, z_send, z_recv, r_send, r_recv):
    me = lax.axis_index(axis)
    team = me // TEAM
    q = me % TEAM
    base = team * TEAM
    odd = q % 2
    teams = n // TEAM
    wins = record.shape[1]
    lags = record.shape[2]
    bins = lags // 2
    chunk = wins // GROUPS
    below = team > 0
    above = team < teams - 1
    step = TEAM * (1 - 2 * odd)
    has_a = jnp.where(odd == 0, team, teams - 1 - team) > 0
    has_b = jnp.where(odd == 0, teams - 1 - team, team) > 0
    sign = (1 - 2 * odd).astype(jnp.float32)

    def block_of(slot):
        return base + jnp.where(odd == 0, slot - 2, 5 - slot)

    barrier = pltpu.get_barrier_semaphore()
    for shift in (-1, 0, 1):
        for i in range(TEAM):
            other = base + shift * TEAM + i
            there = (other >= 0) & (other < n) & (other != me)

            @pl.when(there)
            def _():
                pl.semaphore_signal(barrier, inc=1, device_id={axis: other})
    pl.semaphore_wait(barrier, TEAM - 1 + TEAM * below.astype(jnp.int32) + TEAM * above.astype(jnp.int32))

    def windows(g):
        return pl.ds(g * chunk, chunk)

    def lanes(i):
        return pl.ds(pl.multiple_of(i * LANES, LANES), LANES)

    def trace_copy(peer, g):
        return pltpu.make_async_remote_copy(
            src_ref=traces.at[0, windows(g), :, lanes(peer)],
            dst_ref=record.at[q, windows(g)],
            send_sem=t_send.at[peer, g],
            recv_sem=t_recv.at[q, g],
            device_id={axis: base + peer},
        )

    def own_copy(g):
        return pltpu.make_async_copy(traces.at[0, windows(g), :, lanes(q)], record.at[q, windows(g)], t_recv.at[q, g])

    peers = ((q + 2) % TEAM, 3 - q, q + 1 - 2 * odd)
    for g in range(GROUPS):
        own_copy(g).start()
        for peer in peers:
            trace_copy(peer, g).start()

    def to_a(u, g):
        return pltpu.make_async_remote_copy(
            src_ref=white.at[u + 2, windows(g)],
            dst_ref=white.at[u + 6, windows(g)],
            send_sem=z_send.at[u, g],
            recv_sem=z_recv.at[u + 2, g],
            device_id={axis: me - step},
        )

    def to_b(u, g):
        return pltpu.make_async_remote_copy(
            src_ref=white.at[u + 2, windows(g)],
            dst_ref=white.at[u - 2, windows(g)],
            send_sem=z_send.at[u + 1, g],
            recv_sem=z_recv.at[u - 2, g],
            device_id={axis: me + step},
        )

    def whiten_group(g):
        def one(u, carry):
            i = jnp.where(odd == 0, u, 3 - u)
            pltpu.make_async_copy(record.at[i, windows(g)], record.at[i, windows(g)], t_recv.at[i, g]).wait()
            for h in range(0, chunk, 2):
                w = g * chunk + h
                rec = jnp.concatenate([record[i, w], record[i, w + 1]], axis=1)
                raw = jnp.dot(table_t[...], rec, preferred_element_type=jnp.float32)
                power = jnp.sum(raw * raw, axis=0, keepdims=True) / bins
                inv = 1.0 / jnp.sqrt(power + 1e-06)
                for e in range(2):
                    part = slice(e * LANES, (e + 1) * LANES)
                    keep = mask[base + i, w + e].astype(jnp.float32)
                    white[u + 2, w + e] = (raw[:, part] * (inv[:, part] * keep)).astype(jnp.bfloat16)

            @pl.when((u <= 2) & has_a)
            def _():
                to_a(u, g).start()

            @pl.when((u >= 2) & has_b)
            def _():
                to_b(u, g).start()

            return carry

        lax.fori_loop(0, TEAM, one, 0)

    def stack_run(run, g):
        s, t0, count = run
        first = FIRST[run]

        def one(v, carry):
            t = t0 + v

            def tile(k, inner):
                re_at = pl.ds(pl.multiple_of(k * TILE, TILE), TILE)
                im_at = pl.ds(pl.multiple_of(bins + k * TILE, TILE), TILE)
                fresh = g == 0
                real = jnp.where(fresh, 0.0, acc[first + v, re_at, :])
                imag = jnp.where(fresh, 0.0, acc[first + v, im_at, :])
                for h in range(chunk):
                    w = g * chunk + h
                    a_re = white[s, w, re_at, :].astype(jnp.float32)
                    a_im = white[s, w, im_at, :].astype(jnp.float32)
                    b_re = white[t, w, re_at, :].astype(jnp.float32)
                    b_im = white[t, w, im_at, :].astype(jnp.float32)
                    real = real + (a_re * b_re + a_im * b_im)
                    imag = imag + (a_im * b_re - a_re * b_im)
                acc[first + v, re_at, :] = real
                acc[first + v, im_at, :] = imag
                return inner

            lax.fori_loop(0, bins // TILE, tile, 0)
            return carry

        lax.fori_loop(0, count, one, 0)

    def result_copies(s, t, index):
        early = block_of(jnp.where(odd == 0, s, t))
        late = block_of(jnp.where(odd == 0, t, s))
        out = []
        for side, owner in ((0, early), (1, late)):
            src = res.at[index, pl.ds(side * bins, bins)]
            dst = back.at[side, t - s - 1, :, lanes(q)]
            local = pltpu.make_async_copy(src, dst, r_recv.at[side, t - s - 1])
            remote = pltpu.make_async_remote_copy(
                src_ref=src, dst_ref=dst, send_sem=r_send.at[index, side],
                recv_sem=r_recv.at[side, t - s - 1], device_id={axis: owner},
            )
            out.append((owner, local, remote))
        return out

    def finish_run(run):
        s, t0, count = run
        first = FIRST[run]

        def one(v, carry):
            total = acc[first + v] * (1.0 / math.sqrt(wins))
            stacked = jnp.concatenate([total[:bins], total[bins:] * sign], axis=0).astype(jnp.bfloat16)
            corr = jnp.dot(table_lag[...], stacked, preferred_element_type=jnp.float32) * (1.0 / math.sqrt(bins))
            res[first + v] = corr.astype(jnp.bfloat16)
            for owner, local, remote in result_copies(s, t0 + v, first + v):
                @pl.when(owner == me)
                def _():
                    local.start()

                @pl.when(owner != me)
                def _():
                    remote.start()
            return carry

        lax.fori_loop(0, count, one, 0)

    def finish_sends(run):
        s, t0, count = run
        first = FIRST[run]

        def one(v, carry):
            for owner, local, remote in result_copies(s, t0 + v, first + v):
                @pl.when(owner != me)
                def _():
                    remote.wait_send()
            return carry

        lax.fori_loop(0, count, one, 0)

    def arrived(z, slot, g):
        view = white.at[slot, windows(g)]
        pltpu.make_async_copy(view, view, z_recv.at[z, g]).wait()

    def phase(g, carry):
        @pl.when(g < GROUPS)
        def _():
            whiten_group(g)
            for run in OWN_PAIRS:
                stack_run(run, g)

        @pl.when(g == GROUPS)
        def _():
            for run in OWN_PAIRS:
                finish_run(run)

        @pl.when(g >= 1)
        def _():
            @pl.when(has_a)
            def _():
                for z in range(2):
                    arrived(z, z, g - 1)
                for run in A_PAIRS:
                    stack_run(run, g - 1)

            @pl.when(has_b)
            def _():
                for z in range(2, 5):
                    arrived(z, z + 4, g - 1)
                for run in B_PAIRS:
                    stack_run(run, g - 1)

            @pl.when(has_a & has_b)
            def _():
                for run in AB_PAIRS:
                    stack_run(run, g - 1)

        return carry

    lax.fori_loop(0, GROUPS + 1, phase, 0)

    @pl.when(has_a)
    def _():
        for run in A_PAIRS:
            finish_run(run)

    @pl.when(has_b)
    def _():
        for run in B_PAIRS:
            finish_run(run)

    @pl.when(has_a & has_b)
    def _():
        for run in AB_PAIRS:
            finish_run(run)

    def sent(g, carry):
        for peer in peers:
            trace_copy(peer, g).wait_send()

        @pl.when(has_a)
        def _():
            for u in range(3):
                to_a(u, g).wait_send()

        @pl.when(has_b)
        def _():
            for u in range(2, 4):
                to_b(u, g).wait_send()

        return carry

    lax.fori_loop(0, GROUPS, sent, 0)
    for j in range(MAXP):
        for side, there in ((0, me + j + 1 < n), (1, me - j - 1 >= 0)):
            @pl.when(there)
            def _():
                view = back.at[side, j]
                pltpu.make_async_copy(view, view, r_recv.at[side, j]).wait()
        reach = counts[me] >= j + 1
        fwd_out[0, j] = jnp.where(reach, back[0, j], jnp.bfloat16(0))
        source = jnp.maximum(me - j - 1, 0)
        reached = (counts[source] >= j + 1) & (me >= j + 1)
        bwd_out[0, j] = jnp.where(reached, back[1, j], jnp.bfloat16(0))
    for run in OWN_PAIRS:
        finish_sends(run)

    @pl.when(has_a)
    def _():
        for run in A_PAIRS:
            finish_sends(run)

    @pl.when(has_b)
    def _():
        for run in B_PAIRS:
            finish_sends(run)

    @pl.when(has_a & has_b)
    def _():
        for run in AB_PAIRS:
            finish_sends(run)


def local(traces, mask, counts):
    axis = "chan"
    n = lax.axis_size(axis)
    _, wins, lags, width = traces.shape
    bins = lags // 2
    table = lag_table(lags, bins)
    table_lag = np.concatenate([table[:bins], table[bins:][::-1]], axis=0)
    half = jax.ShapeDtypeStruct((1, MAXP, bins, width), jnp.bfloat16)
    vmem = pl.BlockSpec(memory_space=pltpu.VMEM)
    smem = pl.BlockSpec(memory_space=pltpu.SMEM)
    forward, backward = pl.pallas_call(
        functools.partial(kernel, axis, n),
        out_shape=(half, half),
        in_specs=[pl.BlockSpec(memory_space=pl.ANY), smem, smem, vmem, vmem],
        out_specs=(vmem, vmem),
        scratch_shapes=[
            pltpu.VMEM((TEAM, wins, lags, LANES), jnp.bfloat16),
            pltpu.VMEM((SLOTS, wins, lags, LANES), jnp.bfloat16),
            pltpu.VMEM((PAIRS, lags, LANES), jnp.float32),
            pltpu.VMEM((PAIRS, lags, LANES), jnp.bfloat16),
            pltpu.VMEM((2, MAXP, bins, width), jnp.bfloat16),
            pltpu.SemaphoreType.DMA((TEAM, GROUPS)),
            pltpu.SemaphoreType.DMA((TEAM, GROUPS)),
            pltpu.SemaphoreType.DMA((5, GROUPS)),
            pltpu.SemaphoreType.DMA((5, GROUPS)),
            pltpu.SemaphoreType.DMA((PAIRS, 2)),
            pltpu.SemaphoreType.DMA((2, MAXP)),
        ],
        compiler_params=pltpu.CompilerParams(collective_id=0, has_side_effects=True, vmem_limit_bytes=48 << 20),
        name="xcorr",
    )(traces, mask, counts, jnp.asarray(table.T, jnp.bfloat16), jnp.asarray(table_lag, jnp.bfloat16))
    return forward.astype(jnp.float32), backward.astype(jnp.float32)


def solution(mesh):
    return jax.shard_map(
        local,
        mesh=mesh,
        in_specs=(P(("grp", "chan"), None, None, None), P("grp", None), P("grp")),
        out_specs=(P(("grp", "chan"), None, None, None), P(("grp", "chan"), None, None, None)),
        check_vma=False,
    )
```

time: 476 us -> 90.4 us (0.19)
  the two profiles are of different devices: /device:TPU:5 before, /device:TPU:17 now
where the time goes in v1:
time: 90.4 us; the launch traced here: 88.9 us
  Pallas kernels  80.4 us (89%)
  local copies, waits for them, and re-layouts  5.34 us (6%)
  other arithmetic  2.44 us (3%)
    pallas_call x1, Pallas kernels, local(): pl.pallas_call(functools.partial(kernel, axis, n), out_shape=(half, half)...  80.4 us
    unnamed x10, local copies, waits for them, and re-layouts  5.34 us
    convert_element_type x2, other arithmetic, local(): return (forward.astype(jnp.float32), backward.astype(jnp.float32))  2.44 us

profile of v1, /device:TPU:17, one launch (start us, length us, event | category | flops | bytes accessed | tf_op | source)
XLA Modules:
  0.0 88.9 jit_solution(17754041305022277741)
XLA Ops:
  0.6 0.0 copy-start
  0.6 2.2 %copy-done = bf16[1,16,256,512]{3,2,1,0:T(8,128)(2,1)S(1)} copy-done((bf16[1,16,256,512]{3,2,1,0:T(8,128)(2,1)S(1)}, bf16[1,16,256,512]{3,2,1,0:T(8,128)(2,1)}, u32[]{:S(2)}) %copy-start) | copy-done | bytes 4194328
  2.8 0.0 copy-start.1
  2.8 0.9 %copy-done.1 = bf16[256,256]{1,0:T(8,128)(2,1)S(1)} copy-done((bf16[256,256]{1,0:T(8,128)(2,1)S(1)}, bf16[256,256]{1,0:T(8,128)(2,1)}, u32[]{:S(2)}) %copy-start.1) | copy-done | bytes 131096
  3.7 0.0 copy-start.2
  3.7 0.9 %copy-done.2 = bf16[256,256]{1,0:T(8,128)(2,1)S(1)} copy-done((bf16[256,256]{1,0:T(8,128)(2,1)S(1)}, bf16[256,256]{1,0:T(8,128)(2,1)}, u32[]{:S(2)}) %copy-start.2) | copy-done | bytes 131096
  4.6 0.0 copy-start.3
  4.6 0.7 copy-done.3
  5.3 0.0 copy-start.4
  5.3 0.7 copy-done.4
  6.0 80.4 %xcorr.1 = (bf16[1,5,128,512]{3,2,1,0:T(8,128)(2,1)S(1)}, bf16[1,5,128,512]{3,2,1,0:T(8,128)(2,1)S(1)}) custom-call(bf16[1,16,256,512]{3,2,1,0:T(8,128)(2,1)S(1)} %copy-done, s32[16,16]{1,0:T(8,128)S(1)} %copy-done.3, s32[16]{0:T(128)S(1)} %copy-done.4, bf16[256,256]{1,0:T(8,128)(2,1)S(1)} %copy-done.2, bf16[256,256]{1,0:T(8,128)(2,1)S(1)} %copy-done.1), custom_call_target="tpu_custom_call" | custom-call | tf_op jit(solution)/shard_map/xcorr/pallas_call | solution.py:333
  86.4 1.2 %convert_element_type.6 = f32[1,5,128,512]{3,2,1,0:T(8,128)} convert(bf16[1,5,128,512]{3,2,1,0:T(8,128)(2,1)S(1)} %get-tuple-element.4) | non-fusion elementwise | flops 327680 | bytes 1966080 | tf_op jit(solution)/shard_map/convert_element_type | solution.py:354
  87.7 1.2 %convert_element_type.7 = f32[1,5,128,512]{3,2,1,0:T(8,128)} convert(bf16[1,5,128,512]{3,2,1,0:T(8,128)(2,1)S(1)} %get-tuple-element.5) | non-fusion elementwise | flops 327680 | bytes 1966080 | tf_op jit(solution)/shard_map/convert_element_type | solution.py:354
Async XLA Ops:
  0.6 2.2 %copy-start = (bf16[1,16,256,512]{3,2,1,0:T(8,128)(2,1)S(1)}, bf16[1,16,256,512]{3,2,1,0:T(8,128)(2,1)}, u32[]{:S(2)}) copy-start(bf16[1,16,256,512]{3,2,1,0:T(8,128)(2,1)} %traces.1) | copy-start | bytes 12582916
  2.8 0.9 %copy-start.1 = (bf16[256,256]{1,0:T(8,128)(2,1)S(1)}, bf16[256,256]{1,0:T(8,128)(2,1)}, u32[]{:S(2)}) copy-start(bf16[256,256]{1,0:T(8,128)(2,1)} %constant.5.clone.table_lag) | copy-start | bytes 393220
  3.7 0.9 %copy-start.2 = (bf16[256,256]{1,0:T(8,128)(2,1)S(1)}, bf16[256,256]{1,0:T(8,128)(2,1)}, u32[]{:S(2)}) copy-start(bf16[256,256]{1,0:T(8,128)(2,1)} %constant.4.clone.table_t) | copy-start | bytes 393220
  4.6 0.7 copy-start.3
  5.3 0.7 copy-start.4

commit v2 on v1

--- a/solution.py
+++ b/solution.py
@@ -19,10 +19,11 @@
 
 OWN_PAIRS = [(2, 3, 3), (3, 4, 2), (4, 5, 1)]
 A_PAIRS = [(0, 2, 4), (1, 2, 4)]
-B_PAIRS = [(2, 6, 2), (3, 6, 3)]
+B_PAIRS = [(2, 6, 2), (3, 6, 2)]
+C_PAIRS = [(3, 8, 1)]
 AB_PAIRS = [(1, 6, 1)]
 FIRST = {}
-for _runs in (OWN_PAIRS, A_PAIRS, B_PAIRS, AB_PAIRS):
+for _runs in (OWN_PAIRS, A_PAIRS, B_PAIRS, C_PAIRS, AB_PAIRS):
     for _run in _runs:
         FIRST[_run] = sum(r[2] for r in FIRST)
 PAIRS = sum(r[2] for r in FIRST)
@@ -35,8 +36,8 @@
     return np.concatenate([np.cos(phase), -np.sin(phase)], axis=1)
 
 
-def kernel(axis, n, traces, mask, counts, table_t, table_lag, fwd_out, bwd_out,
-           record, white, acc, res, back,
+def kernel(axis, n, traces, mask_in, counts_in, table_t_in, table_lag_in, fwd_out, bwd_out,
+           mask, counts, table_t, table_lag, fetch, record, white, acc, res, back,
            t_send, t_recv, z_send, z_recv, r_send, r_recv):
     me = lax.axis_index(axis)
     team = me // TEAM
@@ -58,6 +59,15 @@
     def block_of(slot):
         return base + jnp.where(odd == 0, slot - 2, 5 - slot)
 
+    fetches = [
+        pltpu.make_async_copy(src, dst, fetch.at[k])
+        for k, (src, dst) in enumerate(
+            ((table_t_in, table_t), (mask_in, mask), (table_lag_in, table_lag), (counts_in, counts)))
+    ]
+    for copy in fetches:
+        copy.start()
+    early_low = (q % 3) == 0
+    first = jnp.where(early_low, 0, 2)
     barrier = pltpu.get_barrier_semaphore()
     for shift in (-1, 0, 1):
         for i in range(TEAM):
@@ -111,8 +121,9 @@
             device_id={axis: me + step},
         )
 
-    def whiten_group(g):
-        def one(u, carry):
+    def whiten_group(u0, g):
+        def one(v, carry):
+            u = u0 + v
             i = jnp.where(odd == 0, u, 3 - u)
             pltpu.make_async_copy(record.at[i, windows(g)], record.at[i, windows(g)], t_recv.at[i, g]).wait()
             for h in range(0, chunk, 2):
@@ -136,11 +147,11 @@
 
             return carry
 
-        lax.fori_loop(0, TEAM, one, 0)
+        lax.fori_loop(0, 2, one, 0)
 
     def stack_run(run, g):
         s, t0, count = run
-        first = FIRST[run]
+        place = FIRST[run]
 
         def one(v, carry):
             t = t0 + v
@@ -149,8 +160,8 @@
                 re_at = pl.ds(pl.multiple_of(k * TILE, TILE), TILE)
                 im_at = pl.ds(pl.multiple_of(bins + k * TILE, TILE), TILE)
                 fresh = g == 0
-                real = jnp.where(fresh, 0.0, acc[first + v, re_at, :])
-                imag = jnp.where(fresh, 0.0, acc[first + v, im_at, :])
+                real = jnp.where(fresh, 0.0, acc[place + v, re_at, :])
+                imag = jnp.where(fresh, 0.0, acc[place + v, im_at, :])
                 for h in range(chunk):
                     w = g * chunk + h
                     a_re = white[s, w, re_at, :].astype(jnp.float32)
@@ -159,8 +170,8 @@
                     b_im = white[t, w, im_at, :].astype(jnp.float32)
                     real = real + (a_re * b_re + a_im * b_im)
                     imag = imag + (a_im * b_re - a_re * b_im)
-                acc[first + v, re_at, :] = real
-                acc[first + v, im_at, :] = imag
+                acc[place + v, re_at, :] = real
+                acc[place + v, im_at, :] = imag
                 return inner
 
             lax.fori_loop(0, bins // TILE, tile, 0)
@@ -185,14 +196,14 @@
 
     def finish_run(run):
         s, t0, count = run
-        first = FIRST[run]
+        place = FIRST[run]
 
         def one(v, carry):
-            total = acc[first + v] * (1.0 / math.sqrt(wins))
+            total = acc[place + v] * (1.0 / math.sqrt(wins))
             stacked = jnp.concatenate([total[:bins], total[bins:] * sign], axis=0).astype(jnp.bfloat16)
             corr = jnp.dot(table_lag[...], stacked, preferred_element_type=jnp.float32) * (1.0 / math.sqrt(bins))
-            res[first + v] = corr.astype(jnp.bfloat16)
-            for owner, local, remote in result_copies(s, t0 + v, first + v):
+            res[place + v] = corr.astype(jnp.bfloat16)
+            for owner, local, remote in result_copies(s, t0 + v, place + v):
                 @pl.when(owner == me)
                 def _():
                     local.start()
@@ -206,10 +217,10 @@
 
     def finish_sends(run):
         s, t0, count = run
-        first = FIRST[run]
+        place = FIRST[run]
 
         def one(v, carry):
-            for owner, local, remote in result_copies(s, t0 + v, first + v):
+            for owner, local, remote in result_copies(s, t0 + v, place + v):
                 @pl.when(owner != me)
                 def _():
                     remote.wait_send()
@@ -221,57 +232,47 @@
         view = white.at[slot, windows(g)]
         pltpu.make_async_copy(view, view, z_recv.at[z, g]).wait()
 
-    def phase(g, carry):
-        @pl.when(g < GROUPS)
+    def near(g, carry):
+        whiten_group(first, g)
+        return carry
+
+    def far(g, carry):
+        whiten_group(2 - first, g)
+        for run in OWN_PAIRS:
+            stack_run(run, g)
+        return carry
+
+    for copy in fetches[:2]:
+        copy.wait()
+    lax.fori_loop(0, GROUPS, near, 0)
+    lax.fori_loop(0, GROUPS, far, 0)
+    fetches[2].wait()
+    for run in OWN_PAIRS:
+        finish_run(run)
+
+    def group(ready, zs, runs):
+        @pl.when(ready)
         def _():
-            whiten_group(g)
-            for run in OWN_PAIRS:
-                stack_run(run, g)
-
-        @pl.when(g == GROUPS)
-        def _():
-            for run in OWN_PAIRS:
+            def one(g, carry):
+                for z in zs:
+                    arrived(z, z if z < 2 else z + 4, g)
+                for run in runs:
+                    stack_run(run, g)
+                return carry
+
+            lax.fori_loop(0, GROUPS, one, 0)
+            for run in runs:
                 finish_run(run)
 
-        @pl.when(g >= 1)
-        def _():
-            @pl.when(has_a)
-            def _():
-                for z in range(2):
-                    arrived(z, z, g - 1)
-                for run in A_PAIRS:
-                    stack_run(run, g - 1)
-
-            @pl.when(has_b)
-            def _():
-                for z in range(2, 5):
-                    arrived(z, z + 4, g - 1)
-                for run in B_PAIRS:
-                    stack_run(run, g - 1)
-
-            @pl.when(has_a & has_b)
-            def _():
-                for run in AB_PAIRS:
-                    stack_run(run, g - 1)
-
+    def half(p, carry):
+        low = (p == 0) == early_low
+        group(low & has_b, (2, 3), B_PAIRS)
+        group(jnp.logical_not(low) & has_a, (0, 1), A_PAIRS)
+        group(jnp.logical_not(low) & has_b, (4,), C_PAIRS)
         return carry
 
-    lax.fori_loop(0, GROUPS + 1, phase, 0)
-
-    @pl.when(has_a)
-    def _():
-        for run in A_PAIRS:
-            finish_run(run)
-
-    @pl.when(has_b)
-    def _():
-        for run in B_PAIRS:
-            finish_run(run)
-
-    @pl.when(has_a & has_b)
-    def _():
-        for run in AB_PAIRS:
-            finish_run(run)
+    lax.fori_loop(0, 2, half, 0)
+    group(has_a & has_b, (), AB_PAIRS)
 
     def sent(g, carry):
         for peer in peers:
@@ -290,6 +291,7 @@
         return carry
 
     lax.fori_loop(0, GROUPS, sent, 0)
+    fetches[3].wait()
     for j in range(MAXP):
         for side, there in ((0, me + j + 1 < n), (1, me - j - 1 >= 0)):
             @pl.when(there)
@@ -311,7 +313,7 @@
 
     @pl.when(has_b)
     def _():
-        for run in B_PAIRS:
+        for run in B_PAIRS + C_PAIRS:
             finish_sends(run)
 
     @pl.when(has_a & has_b)
@@ -329,13 +331,17 @@
     table_lag = np.concatenate([table[:bins], table[bins:][::-1]], axis=0)
     half = jax.ShapeDtypeStruct((1, MAXP, bins, width), jnp.bfloat16)
     vmem = pl.BlockSpec(memory_space=pltpu.VMEM)
-    smem = pl.BlockSpec(memory_space=pltpu.SMEM)
     forward, backward = pl.pallas_call(
         functools.partial(kernel, axis, n),
         out_shape=(half, half),
-        in_specs=[pl.BlockSpec(memory_space=pl.ANY), smem, smem, vmem, vmem],
+        in_specs=[pl.BlockSpec(memory_space=pltpu.HBM)] * 5,
         out_specs=(vmem, vmem),
         scratch_shapes=[
+            pltpu.SMEM(mask.shape, jnp.int32),
+            pltpu.SMEM(counts.shape, jnp.int32),
+            pltpu.VMEM((lags, lags), jnp.bfloat16),
+            pltpu.VMEM((lags, lags), jnp.bfloat16),
+            pltpu.SemaphoreType.DMA((4,)),
             pltpu.VMEM((TEAM, wins, lags, LANES), jnp.bfloat16),
             pltpu.VMEM((SLOTS, wins, lags, LANES), jnp.bfloat16),
             pltpu.VMEM((PAIRS, lags, LANES), jnp.float32),
@@ -348,7 +354,7 @@
             pltpu.SemaphoreType.DMA((PAIRS, 2)),
             pltpu.SemaphoreType.DMA((2, MAXP)),
         ],
-        compiler_params=pltpu.CompilerParams(collective_id=0, has_side_effects=True, vmem_limit_bytes=48 << 20),
+        compiler_params=pltpu.CompilerParams(collective_id=0, has_side_effects=True, vmem_limit_bytes=60 << 20),
         name="xcorr",
     )(traces, mask, counts, jnp.asarray(table.T, jnp.bfloat16), jnp.asarray(table_lag, jnp.bfloat16))
     return forward.astype(jnp.float32), backward.astype(jnp.float32)

time: 90.4 us -> 77.2 us (0.85); the launches traced: 88.9 us -> 77.1 us
  Pallas kernels: 80.4 us -> 72.8 us
  local copies, waits for them, and re-layouts: 5.34 us -> 0.01 us
  other arithmetic: 2.44 us -> 3.61 us
    pallas_call x1, Pallas kernels: 80.4 us -> 72.8 us  [local(): pl.pallas_call(functools.partial(kernel, axis, n), out_shape=(half, half)...]
    unnamed x10 -> x2, local copies, waits for them, and re-layouts: 5.34 us -> 0.01 us
    convert_element_type x2, other arithmetic: 2.44 us -> 3.61 us  [local(): return (forward.astype(jnp.float32), backward.astype(jnp.float32))]
where the time goes in v2:
time: 77.2 us; the launch traced here: 77.1 us
  Pallas kernels  72.8 us (94%)
  other arithmetic  3.61 us (5%)
    pallas_call x1, Pallas kernels, local(): pl.pallas_call(functools.partial(kernel, axis, n), out_shape=(half, half)...  72.8 us
    convert_element_type x2, other arithmetic, local(): return (forward.astype(jnp.float32), backward.astype(jnp.float32))  3.61 us

profile of v2, /device:TPU:17, one launch (start us, length us, event | category | flops | bytes accessed | tf_op | source)
XLA Modules:
  0.0 77.1 jit_solution(11176383694637504541)
XLA Ops:
  0.6 72.8 %xcorr.1 = (bf16[1,5,128,512]{3,2,1,0:T(8,128)(2,1)}, bf16[1,5,128,512]{3,2,1,0:T(8,128)(2,1)}) custom-call(bf16[1,16,256,512]{3,2,1,0:T(8,128)(2,1)} %traces.1, s32[16,16]{1,0:T(8,128)} %mask_in.1, s32[16]{0:T(128)} %counts_in.1, bf16[256,256]{1,0:T(8,128)(2,1)} %constant.4.clone.table_t_in, bf16[256,256]{1,0:T(8,128)(2,1)} %constant.5.clone.table_lag_in), custom_call_target="tpu_custom_call" | custom-call | tf_op jit(solution)/shard_map/xcorr/pallas_call | solution.py:334
  73.5 0.0 copy-start
  73.5 2.4 %convert_element_type.6 = f32[1,5,128,512]{3,2,1,0:T(8,128)} convert(bf16[1,5,128,512]{3,2,1,0:T(8,128)(2,1)} %get-tuple-element.4) | non-fusion elementwise | flops 327680 | bytes 1966080 | tf_op jit(solution)/shard_map/convert_element_type | solution.py:360
  75.8 0.0 copy-done
  75.8 1.2 %convert_element_type.7 = f32[1,5,128,512]{3,2,1,0:T(8,128)} convert(bf16[1,5,128,512]{3,2,1,0:T(8,128)(2,1)S(1)} %copy-done) | non-fusion elementwise | flops 327680 | bytes 1966080 | tf_op jit(solution)/shard_map/convert_element_type | solution.py:360
Async XLA Ops:
  73.5 2.4 %copy-start = (bf16[1,5,128,512]{3,2,1,0:T(8,128)(2,1)S(1)}, bf16[1,5,128,512]{3,2,1,0:T(8,128)(2,1)}, u32[]{:S(2)}) copy-start(bf16[1,5,128,512]{3,2,1,0:T(8,128)(2,1)} %get-tuple-element.5) | copy-start | bytes 1966084

commit v3 on v2

--- a/solution.py
+++ b/solution.py
@@ -16,6 +16,7 @@
 GROUPS = 4
 SLOTS = 9
 TILE = 32
+SPAN = 5
 
 OWN_PAIRS = [(2, 3, 3), (3, 4, 2), (4, 5, 1)]
 A_PAIRS = [(0, 2, 4), (1, 2, 4)]
@@ -38,7 +39,7 @@
 
 def kernel(axis, n, traces, mask_in, counts_in, table_t_in, table_lag_in, fwd_out, bwd_out,
            mask, counts, table_t, table_lag, fetch, record, white, acc, res, back,
-           t_send, t_recv, z_send, z_recv, r_send, r_recv):
+           ready, o_sem, t_send, t_recv, z_send, z_recv, r_send, r_recv):
     me = lax.axis_index(axis)
     team = me // TEAM
     q = me % TEAM
@@ -77,7 +78,6 @@
             @pl.when(there)
             def _():
                 pl.semaphore_signal(barrier, inc=1, device_id={axis: other})
-    pl.semaphore_wait(barrier, TEAM - 1 + TEAM * below.astype(jnp.int32) + TEAM * above.astype(jnp.int32))
 
     def windows(g):
         return pl.ds(g * chunk, chunk)
@@ -100,8 +100,6 @@
     peers = ((q + 2) % TEAM, 3 - q, q + 1 - 2 * odd)
     for g in range(GROUPS):
         own_copy(g).start()
-        for peer in peers:
-            trace_copy(peer, g).start()
 
     def to_a(u, g):
         return pltpu.make_async_remote_copy(
@@ -121,33 +119,38 @@
             device_id={axis: me + step},
         )
 
-    def whiten_group(u0, g):
-        def one(v, carry):
-            u = u0 + v
-            i = jnp.where(odd == 0, u, 3 - u)
-            pltpu.make_async_copy(record.at[i, windows(g)], record.at[i, windows(g)], t_recv.at[i, g]).wait()
-            for h in range(0, chunk, 2):
-                w = g * chunk + h
-                rec = jnp.concatenate([record[i, w], record[i, w + 1]], axis=1)
-                raw = jnp.dot(table_t[...], rec, preferred_element_type=jnp.float32)
-                power = jnp.sum(raw * raw, axis=0, keepdims=True) / bins
-                inv = 1.0 / jnp.sqrt(power + 1e-06)
-                for e in range(2):
-                    part = slice(e * LANES, (e + 1) * LANES)
-                    keep = mask[base + i, w + e].astype(jnp.float32)
-                    white[u + 2, w + e] = (raw[:, part] * (inv[:, part] * keep)).astype(jnp.bfloat16)
-
-            @pl.when((u <= 2) & has_a)
-            def _():
-                to_a(u, g).start()
-
-            @pl.when((u >= 2) & has_b)
-            def _():
-                to_b(u, g).start()
-
+    own_slot = jnp.where(odd == 0, q, 3 - q)
+
+    def whiten_block(u, g):
+        i = jnp.where(odd == 0, u, 3 - u)
+        pltpu.make_async_copy(record.at[i, windows(g)], record.at[i, windows(g)], t_recv.at[i, g]).wait()
+        for h in range(0, chunk, 2):
+            w = g * chunk + h
+            rec = jnp.concatenate([record[i, w], record[i, w + 1]], axis=1)
+            raw = jnp.dot(table_t[...], rec, preferred_element_type=jnp.float32)
+            power = jnp.sum(raw * raw, axis=0, keepdims=True) / bins
+            inv = 1.0 / jnp.sqrt(power + 1e-06)
+            for e in range(2):
+                part = slice(e * LANES, (e + 1) * LANES)
+                keep = mask[base + i, w + e].astype(jnp.float32)
+                white[u + 2, w + e] = (raw[:, part] * (inv[:, part] * keep)).astype(jnp.bfloat16)
+
+    def pass_on(u, g):
+        @pl.when((u <= 2) & has_a)
+        def _():
+            to_a(u, g).start()
+
+        @pl.when((u >= 2) & has_b)
+        def _():
+            to_b(u, g).start()
+
+    def block_chunks(u, start):
+        def one(g, carry):
+            whiten_block(u, g)
+            pass_on(u, g)
             return carry
 
-        lax.fori_loop(0, 2, one, 0)
+        lax.fori_loop(start, GROUPS, one, 0)
 
     def stack_run(run, g):
         s, t0, count = run
@@ -232,19 +235,24 @@
         view = white.at[slot, windows(g)]
         pltpu.make_async_copy(view, view, z_recv.at[z, g]).wait()
 
-    def near(g, carry):
-        whiten_group(first, g)
-        return carry
-
     def far(g, carry):
-        whiten_group(2 - first, g)
+        for v in range(2):
+            whiten_block(2 - first + v, g)
+            pass_on(2 - first + v, g)
         for run in OWN_PAIRS:
             stack_run(run, g)
         return carry
 
     for copy in fetches[:2]:
         copy.wait()
-    lax.fori_loop(0, GROUPS, near, 0)
+    whiten_block(own_slot, 0)
+    pl.semaphore_wait(barrier, TEAM - 1 + TEAM * below.astype(jnp.int32) + TEAM * above.astype(jnp.int32))
+    pass_on(own_slot, 0)
+    for g in range(GROUPS):
+        for peer in peers:
+            trace_copy(peer, g).start()
+    block_chunks(own_slot, 1)
+    block_chunks(2 * first + 1 - own_slot, 0)
     lax.fori_loop(0, GROUPS, far, 0)
     fetches[2].wait()
     for run in OWN_PAIRS:
@@ -299,10 +307,12 @@
                 view = back.at[side, j]
                 pltpu.make_async_copy(view, view, r_recv.at[side, j]).wait()
         reach = counts[me] >= j + 1
-        fwd_out[0, j] = jnp.where(reach, back[0, j], jnp.bfloat16(0))
+        ready[0, j] = jnp.where(reach, back[0, j], jnp.bfloat16(0))
+        pltpu.make_async_copy(ready.at[0, j], fwd_out.at[0, j], o_sem.at[0, j]).start()
         source = jnp.maximum(me - j - 1, 0)
         reached = (counts[source] >= j + 1) & (me >= j + 1)
-        bwd_out[0, j] = jnp.where(reached, back[1, j], jnp.bfloat16(0))
+        ready[1, j] = jnp.where(reached, back[1, j], jnp.bfloat16(0))
+        pltpu.make_async_copy(ready.at[1, j], bwd_out.at[0, j], o_sem.at[1, j]).start()
     for run in OWN_PAIRS:
         finish_sends(run)
 
@@ -320,6 +330,14 @@
     def _():
         for run in AB_PAIRS:
             finish_sends(run)
+    for j in range(MAXP):
+        pltpu.make_async_copy(ready.at[0, j], fwd_out.at[0, j], o_sem.at[0, j]).wait()
+        pltpu.make_async_copy(ready.at[1, j], bwd_out.at[0, j], o_sem.at[1, j]).wait()
+
+
+def widen(fwd, bwd, fwd_out, bwd_out):
+    fwd_out[...] = fwd[...].astype(jnp.float32)
+    bwd_out[...] = bwd[...].astype(jnp.float32)
 
 
 def local(traces, mask, counts):
@@ -330,12 +348,11 @@
     table = lag_table(lags, bins)
     table_lag = np.concatenate([table[:bins], table[bins:][::-1]], axis=0)
     half = jax.ShapeDtypeStruct((1, MAXP, bins, width), jnp.bfloat16)
-    vmem = pl.BlockSpec(memory_space=pltpu.VMEM)
     forward, backward = pl.pallas_call(
         functools.partial(kernel, axis, n),
         out_shape=(half, half),
         in_specs=[pl.BlockSpec(memory_space=pltpu.HBM)] * 5,
-        out_specs=(vmem, vmem),
+        out_specs=[pl.BlockSpec(memory_space=pltpu.HBM)] * 2,
         scratch_shapes=[
             pltpu.SMEM(mask.shape, jnp.int32),
             pltpu.SMEM(counts.shape, jnp.int32),
@@ -347,6 +364,8 @@
             pltpu.VMEM((PAIRS, lags, LANES), jnp.float32),
             pltpu.VMEM((PAIRS, lags, LANES), jnp.bfloat16),
             pltpu.VMEM((2, MAXP, bins, width), jnp.bfloat16),
+            pltpu.VMEM((2, MAXP, bins, width), jnp.bfloat16),
+            pltpu.SemaphoreType.DMA((2, MAXP)),
             pltpu.SemaphoreType.DMA((TEAM, GROUPS)),
             pltpu.SemaphoreType.DMA((TEAM, GROUPS)),
             pltpu.SemaphoreType.DMA((5, GROUPS)),
@@ -357,7 +376,16 @@
         compiler_params=pltpu.CompilerParams(collective_id=0, has_side_effects=True, vmem_limit_bytes=60 << 20),
         name="xcorr",
     )(traces, mask, counts, jnp.asarray(table.T, jnp.bfloat16), jnp.asarray(table_lag, jnp.bfloat16))
-    return forward.astype(jnp.float32), backward.astype(jnp.float32)
+    lag_block = pl.BlockSpec((1, SPAN, bins, width), lambda j: (0, j, 0, 0))
+    wide = jax.ShapeDtypeStruct(half.shape, jnp.float32)
+    return pl.pallas_call(
+        widen,
+        grid=(MAXP // SPAN,),
+        out_shape=(wide, wide),
+        in_specs=[lag_block, lag_block],
+        out_specs=(lag_block, lag_block),
+        name="widen",
+    )(forward, backward)
 
 
 def solution(mesh):

time: 77.2 us -> 76 us (0.984)
  other arithmetic: 3.61 us -> 0 us
  Pallas kernels: 72.8 us -> 75.2 us
    convert_element_type x2 -> x0, other arithmetic: 3.61 us -> none  [local(): return (forward.astype(jnp.float32), backward.astype(jnp.float32))]
    pallas_call x0 -> x1, Pallas kernels: none -> 2.86 us  [local(): pl.pallas_call(widen, grid=(MAXP // SPAN,), out_shape=(wide, wide), in_sp...]
where the time goes in v3:
time: 76 us; the launch traced here: 75.8 us
  Pallas kernels  75.2 us (99%)
    pallas_call x1, Pallas kernels, local(): pl.pallas_call(functools.partial(kernel, axis, n), out_shape=(half, half)...  72.3 us
    pallas_call x1, Pallas kernels, local(): pl.pallas_call(widen, grid=(MAXP // SPAN,), out_shape=(wide, wide), in_sp...  2.86 us

profile of v3, /device:TPU:17, one launch (start us, length us, event | category | flops | bytes accessed | tf_op | source)
XLA Modules:
  0.0 75.8 jit_solution(1455292550068659359)
XLA Ops:
  0.6 72.3 %xcorr.1 = (bf16[1,5,128,512]{3,2,1,0:T(8,128)(2,1)}, bf16[1,5,128,512]{3,2,1,0:T(8,128)(2,1)}) custom-call(bf16[1,16,256,512]{3,2,1,0:T(8,128)(2,1)} %traces.1, s32[16,16]{1,0:T(8,128)} %mask_in.1, s32[16]{0:T(128)} %counts_in.1, bf16[256,256]{1,0:T(8,128)(2,1)} %constant.4.clone.table_t_in, bf16[256,256]{1,0:T(8,128)(2,1)} %constant.5.clone.table_lag_in), custom_call_target="tpu_custom_call" | custom-call | tf_op jit(solution)/shard_map/xcorr/pallas_call | solution.py:351
  73.0 2.9 %widen.1 = (f32[1,5,128,512]{3,2,1,0:T(8,128)}, f32[1,5,128,512]{3,2,1,0:T(8,128)}) custom-call(bf16[1,5,128,512]{3,2,1,0:T(8,128)(2,1)} %get-tuple-element.4.fwd, bf16[1,5,128,512]{3,2,1,0:T(8,128)(2,1)} %get-tuple-element.5.bwd), custom_call_target="tpu_custom_call" | custom-call | tf_op jit(solution)/shard_map/widen/pallas_call | solution.py:381

commit v4 on v3

--- a/solution.py
+++ b/solution.py
@@ -266,11 +266,13 @@
                     arrived(z, z if z < 2 else z + 4, g)
                 for run in runs:
                     stack_run(run, g)
+
+                    @pl.when(g == GROUPS - 1)
+                    def _():
+                        finish_run(run)
                 return carry
 
             lax.fori_loop(0, GROUPS, one, 0)
-            for run in runs:
-                finish_run(run)
 
     def half(p, carry):
         low = (p == 0) == early_low

time: 76 us -> 75.6 us (level)
  no operation moved by 1% of the time
where the time goes in v4:
time: 75.6 us; the launch traced here: 75.4 us
  Pallas kernels  74.8 us (99%)
    pallas_call x1, Pallas kernels, local(): pl.pallas_call(functools.partial(kernel, axis, n), out_shape=(half, half)...  71.9 us
    pallas_call x1, Pallas kernels, local(): pl.pallas_call(widen, grid=(MAXP // SPAN,), out_shape=(wide, wide), in_sp...  2.86 us

profile of v4, /device:TPU:17, one launch (start us, length us, event | category | flops | bytes accessed | tf_op | source)
XLA Modules:
  0.0 75.4 jit_solution(323629237428759456)
XLA Ops:
  0.6 71.9 %xcorr.1 = (bf16[1,5,128,512]{3,2,1,0:T(8,128)(2,1)}, bf16[1,5,128,512]{3,2,1,0:T(8,128)(2,1)}) custom-call(bf16[1,16,256,512]{3,2,1,0:T(8,128)(2,1)} %traces.1, s32[16,16]{1,0:T(8,128)} %mask_in.1, s32[16]{0:T(128)} %counts_in.1, bf16[256,256]{1,0:T(8,128)(2,1)} %constant.4.clone.table_t_in, bf16[256,256]{1,0:T(8,128)(2,1)} %constant.5.clone.table_lag_in), custom_call_target="tpu_custom_call" | custom-call | tf_op jit(solution)/shard_map/xcorr/pallas_call | solution.py:353
  72.5 2.9 %widen.1 = (f32[1,5,128,512]{3,2,1,0:T(8,128)}, f32[1,5,128,512]{3,2,1,0:T(8,128)}) custom-call(bf16[1,5,128,512]{3,2,1,0:T(8,128)(2,1)} %get-tuple-element.4.fwd, bf16[1,5,128,512]{3,2,1,0:T(8,128)(2,1)} %get-tuple-element.5.bwd), custom_call_target="tpu_custom_call" | custom-call | tf_op jit(solution)/shard_map/widen/pallas_call | solution.py:383
